TPU v7x, 256 devices: a whole 4x4x8 slice. The times are simulated.
256 devices in a mesh: pole: 8 (over x, y_lo), sub: 32 (over y_hi, z, core).
Axes of the slice: x: 4, y: 4 (y_hi: 2, y_lo: 2; y = y_hi * 2 + y_lo), z: 8, core: 2. Of those that a mesh axis runs over, the one named last changes fastest.
Arguments:
- start_block: float32 [131072, 128], P('sub'), may hold values from -400 to 400
- inverses: float32 [8, 256, 512, 512], P('pole', 'sub'), may hold values from -1 to 3
- iface_rows: int32 [256, 2, 128], P('sub'), may hold values from 0 to 511, as said below
- neighbors: int32 [256, 2], P('sub'), may hold values from 0 to 255, as said below
- couplings: float32 [256, 2, 128], P('sub'), may hold values from 0.25 to 1
- pole_weights: float32 [8], P('pole'), may hold values from 0.25 to 1
Outputs:
- ortho_basis: float32 [131072, 128], P(('sub', 'pole'))
Inputs may be any that keep to these rules, and one draw needn't show every extreme that they name: `iface_rows`: in each subdomain the 256 listed rows are distinct. Subdomain j lies on index j // 8 of sub. neighbors[j, 0] lies on the previous index and neighbors[j, 1] on the next one, cyclically; over the subdomains of one index, the values in column 0 are the previous index's 8 subdomains, each once, and those in column 1 the next index's, each once.
All inputs are finite; a program needn't handle non-finite values.
Results may differ from a plain program's by a relative error of at most 0.0002.
Values sent between devices are 32-bit elements; how exact they have to be, the bound alone decides.
A program may use at most 64 MiB of HBM per device.

v0:
```python
import math
import jax
import jax.numpy as jnp
from jax import lax
from jax.sharding import PartitionSpec as P

precise = lax.Precision.HIGHEST


def extended_2(cells, sides, width):
    for axis, dim in sides:
        count = lax.axis_size(axis)
        head = lax.slice_in_dim(cells, 0, width, axis=dim)
        tail = lax.slice_in_dim(cells, cells.shape[dim] - width, cells.shape[dim], axis=dim)
        cells = jnp.concatenate(
            [
                lax.ppermute(tail, axis, [(i, (i + 1) % count) for i in range(count)]),
                cells,
                lax.ppermute(head, axis, [((i + 1) % count, i) for i in range(count)]),
            ],
            axis=dim,
        )
    return cells


def apply_blocks(blocks, fields):
    return jnp.einsum(
        "sij,sjv->siv", blocks, fields, precision=precise, preferred_element_type=jnp.float32
    )


def add_coupled(fields, iface_rows, neighbor_vals, couplings):

    def one_sub(field_one, rows_one, terms_one):
        field_one = field_one.at[rows_one[0]].add(terms_one[0])
        return field_one.at[rows_one[1]].add(terms_one[1])

    return jax.vmap(one_sub)(fields, iface_rows, couplings[..., None] * neighbor_vals)


def per_device(start_block, inverses, iface_rows, neighbors, couplings, pole_weights):
    blocks = inverses[0]
    sub_count = blocks.shape[0]
    block_len = blocks.shape[1]
    vec_count = start_block.shape[1]
    iface_len = iface_rows.shape[2]
    fields = start_block.reshape(sub_count, block_len, vec_count)
    first_pass = apply_blocks(blocks, fields)
    offsets = (jnp.arange(sub_count, dtype=jnp.int32) * block_len)[:, None, None]
    flat_index = (iface_rows + offsets).transpose(1, 0, 2).reshape(-1)
    outgoing = jnp.take(first_pass.reshape(sub_count * block_len, vec_count), flat_index, axis=0)
    half_rows = sub_count * iface_len
    extended = extended_2(outgoing, (("sub", 0),), half_rows)
    from_prev = extended[:half_rows].reshape(sub_count, iface_len, vec_count)
    from_next = extended[3 * half_rows :].reshape(sub_count, iface_len, vec_count)
    columns = jnp.arange(sub_count, dtype=jnp.int32)[None, :]
    choose_prev = (neighbors[:, 0:1] % sub_count == columns).astype(jnp.float32)
    choose_next = (neighbors[:, 1:2] % sub_count == columns).astype(jnp.float32)
    low_terms = jnp.einsum(
        "jk,kiv->jiv", choose_prev, from_prev, precision=precise, preferred_element_type=jnp.float32
    )
    high_terms = jnp.einsum(
        "jk,kiv->jiv", choose_next, from_next, precision=precise, preferred_element_type=jnp.float32
    )
    corrected = add_coupled(fields, iface_rows, jnp.stack([low_terms, high_terms], 1), couplings)
    weight = pole_weights[0]
    own_rows = sub_count * block_len // lax.axis_size("pole")
    pole_term = weight * apply_blocks(blocks, corrected).reshape(sub_count * block_len, vec_count)
    summed_poles = lax.psum(pole_term, "pole")
    filtered = lax.dynamic_slice_in_dim(
        summed_poles, lax.axis_index("pole") * own_rows, own_rows, 0
    )
    local_gram = jnp.dot(
        filtered.T, filtered, precision=precise, preferred_element_type=jnp.float32
    )
    gram_matrix = lax.psum(local_gram, ("pole", "sub"))
    lower_factor = jnp.linalg.cholesky(gram_matrix)
    total_rows = sub_count * block_len * lax.axis_size("sub")
    solved = lax.linalg.triangular_solve(
        lower_factor, filtered, left_side=False, lower=True, transpose_a=True
    )
    return math.sqrt(total_rows) * solved


def solution(mesh):
    placed = (
        P("sub", None),
        P("pole", "sub", None, None),
        P("sub", None, None),
        P("sub", None),
        P("sub", None, None),
        P("pole"),
    )
    return jax.shard_map(
        per_device, mesh=mesh, in_specs=placed, out_specs=P(("sub", "pole"), None), check_vma=False
    )
```

profile of v0, /device:TPU:1, one launch (start us, length us, event | category | flops | bytes accessed | tf_op | source)
XLA Modules:
  0.0 464.7 jit_solution(7205133361967697777)
XLA Ops:
  6.5 0.0 all-reduce.3.cloned.1.call-start
  6.5 1.6 copy.37
  8.1 0.0 copy-done
  8.1 0.1 compare_and_fusion
  8.3 10.6 %fusion.2 = f32[8,512,128]{2,1,0:T(8,128)} fusion(f32[8,512,128]{2,1,0:T(8,128)S(1)} %bitcast.62, f32[1,8,512,512]{3,2,1,0:T(8,128)} %param.7), kind=kOutput, calls=%fused_computation.5 | convolution fusion | flops 3221225472 | bytes 12582912 | tf_op jit(solution)/shard_map/sij,sjv->siv/dot_general | solution.py:27
  18.8 7.0 %gather_fusion = f32[2048,128]{1,0:T(8,128)S(1)} fusion(f32[4096,128]{1,0:T(8,128)} %bitcast.64, s32[2048]{0:T(1024)S(1)} %broadcast_clamp_fusion), kind=kCustom, calls=%fused_computation | custom fusion | bytes 2105344 | tf_op jit(solution)/shard_map/jit(_take)/gather | solution.py:51
  25.9 0.0 slice-start
  25.9 0.0 copy-start.2
  25.9 0.0 copy-start.3
  25.9 0.0 copy-start.1
  25.9 0.0 copy-start.4
  25.9 0.3 broadcast_select_fusion
  26.3 1.1 fusion.27
  27.3 3.2 collective-permute-start.1
  30.5 0.0 collective-permute-start
  30.6 0.0 slice-done
  30.6 0.0 copy-done.2
  30.6 0.0 copy-done.3
  30.6 0.1 multiply_reduce_fusion
  30.7 0.0 copy-done.1
  30.7 0.1 copy.12
  31.5 0.0 copy-done.4
  31.5 0.1 and_reduce_fusion
  31.6 5.8 %collective-permute-done.1 = f32[1024,128]{1,0:T(8,128)S(1)} collective-permute-done((f32[1024,128]{1,0:T(8,128)}, f32[1024,128]{1,0:T(8,128)S(1)}, u32[]{:S(2)}, u32[]{:S(2)}) %collective-permute-start.1) | collective-permute-done | bytes 524320 | tf_op jit(solution)/shard_map/ppermute | solution.py:19
  37.4 0.7 convolution_bitcast_fusion
  38.1 0.3 collective-permute-done
  38.4 0.7 convolution_bitcast_fusion.1
  39.0 0.3 maximum_multiply_fusion
  39.4 0.1 fusion.26
  39.5 0.1 copy.16
  39.6 0.1 copy.18
  39.7 6.8 %scatter_fusion = f32[4096,128]{1,0:T(8,128)S(1)} fusion(f32[4096,128]{1,0:T(8,128)S(1)} %copy.37, s32[1024]{0:T(1024)S(1)} %get-tuple-element.18, f32[1024,128]{1,0:T(8,128)S(1)} %bitcast.67), kind=kCustom, calls=%fused_computation.1 | custom fusion | flops 131072 | bytes 1576960
  46.5 7.0 %scatter_fusion.1 = f32[4096,128]{1,0:T(8,128)S(1)} fusion(f32[4096,128]{1,0:T(8,128)S(1)} %scatter_fusion, s32[1024]{0:T(1024)S(1)} %get-tuple-element.17, f32[1024,128]{1,0:T(8,128)S(1)} %bitcast.66), kind=kCustom, calls=%fused_computation.2 | custom fusion | flops 131072 | bytes 1576960
  53.5 12.6 %multiply_bitcast_fusion = f32[8,512,128]{1,2,0:T(8,128)} fusion(f32[8,512,128]{2,1,0:T(8,128)S(1)} %bitcast.63, f32[1,8,512,512]{3,2,1,0:T(8,128)} %param.7, f32[]{:T(128)} %bitcast.61), kind=kOutput, calls=%fused_computation.7 | convolution fusion | flops 3221749760 | bytes 12582916 | tf_op jit(solution)/shard_map/sij,sjv->siv/dot_general | solution.py:27
  66.1 2.9 copy.20
  69.0 0.0 all-reduce.3.cloned.1.call-update
  69.0 0.0 all-reduce.5.cloned.1.call-start
  69.1 113.2 %all-reduce.3.cloned.1.call-done = f32[4096,128]{1,0:T(8,128)} async-done(((f32[4096,128]{1,0:T(8,128)}), f32[4096,128]{1,0:T(8,128)}) %all-reduce.3.cloned.1.call-update) | async-done | bytes 2097168 | tf_op jit(solution)/shard_map/psum | solution.py:69
  182.3 2.2 fusion.9
  184.6 0.0 all-reduce.5.cloned.1.call-update
  184.6 246.6 %all-reduce.5.cloned.1.call-done = f32[128,128]{0,1:T(8,128)} async-done(((f32[128,128]{0,1:T(8,128)}), f32[128,128]{0,1:T(8,128)}) %all-reduce.5.cloned.1.call-update) | async-done | bytes 65552 | tf_op jit(solution)/shard_map/psum | solution.py:76
  431.2 0.9 copy.22
  432.1 0.9 fusion.13
  433.0 11.7 %cholesky.16 = f32[128,128]{1,0:T(8,128)S(1)} custom-call(f32[128,128]{1,0:T(8,128)S(1)} %fusion.13), custom_call_target="Cholesky" | custom-call | tf_op jit(solution)/shard_map/jit(cholesky)/cholesky | solution.py:77
  444.8 0.6 compare_reduce_fusion
  445.4 0.7 fusion.11
  446.1 9.8 %custom-call.6 = f32[1,128,128]{1,2,0:T(8,128)S(1)} custom-call(f32[1,128,128]{2,1,0:T(8,128)S(1)} %fusion.11), custom_call_target="InvertDiagBlocksLowerTriangular" | custom-call | tf_op jit(solution)/shard_map/triangular_solve | solution.py:79
  455.9 2.0 convolution_multiply_fusion
  (11 shorter events, 0.1 us)
Async XLA Ops:
  6.5 1.6 copy-start
  6.5 175.8 %all-reduce.3.cloned.1.call-start = ((), (), s32[]{:S(2)}) async-start(), calls=%async_computation | async-start | bytes 4194304 | tf_op jit(solution)/shard_map/psum | solution.py:69
  25.9 4.7 %slice-start = ((s32[8,2,128]{2,1,0:T(2,128)}), s32[8,1,128]{2,1,0:T(1,128)S(1)}, s32[]{:S(2)}) async-start(s32[8,2,128]{2,1,0:T(2,128)} %param.8), calls=%async_computation.2 | async-start | bytes 8192 | tf_op jit(solution)/shard_map/vmap()/slice | solution.py:35
  25.9 4.7 %copy-start.2 = (s32[8,2]{0,1:T(2,128)S(1)}, s32[8,2]{0,1:T(2,128)}, u32[]{:S(2)}) copy-start(s32[8,2]{0,1:T(2,128)} %param.9) | copy-start | bytes 196
  25.9 4.7 %copy-start.3 = (s32[2]{0:T(128)S(1)}, s32[2]{0:T(128)}, u32[]{:S(2)}) copy-start(s32[2]{0:T(128)} %constant.95) | copy-start | bytes 28
  25.9 4.8 %copy-start.1 = (f32[8,2,128]{2,1,0:T(2,128)S(1)}, f32[8,2,128]{2,1,0:T(2,128)}, u32[]{:S(2)}) copy-start(f32[8,2,128]{2,1,0:T(2,128)} %param.10) | copy-start | bytes 24580
  25.9 5.6 %copy-start.4 = (s32[2]{0:T(128)S(1)}, s32[2]{0:T(128)}, u32[]{:S(2)}) copy-start(s32[2]{0:T(128)} %constant.98) | copy-start | bytes 28
  27.3 10.1 %collective-permute-start.1 = (f32[1024,128]{1,0:T(8,128)}, f32[1024,128]{1,0:T(8,128)S(1)}, u32[]{:S(2)}, u32[]{:S(2)}) collective-permute-start(f32[1024,128]{1,0:T(8,128)} %get-tuple-element.14), channel_id=1, source_target_pairs={{1,0},{2,1},{3,2},{4,3},{5,4},{6,5},{7,6},{8,7},{9,8},{10,9},{11,1... | collective-permute-start | bytes 1572872 | tf_op jit(solution)/shard_map/ppermute | solution.py:19
  30.5 7.8 %collective-permute-start = (f32[1024,128]{1,0:T(8,128)}, f32[1024,128]{1,0:T(8,128)S(1)}, u32[]{:S(2)}, u32[]{:S(2)}) collective-permute-start(f32[1024,128]{1,0:T(8,128)} %get-tuple-element.13), channel_id=1, source_target_pairs={{0,1},{1,2},{2,3},{3,4},{4,5},{5,6},{6,7},{7,8},{8,9},{9,10},{10,1... | collective-permute-start | bytes 1572872 | tf_op jit(solution)/shard_map/ppermute | solution.py:17
  69.0 362.2 %all-reduce.5.cloned.1.call-start = ((), (), s32[]{:S(2)}) async-start(), calls=%async_computation.1 | async-start | bytes 131072 | tf_op jit(solution)/shard_map/psum | solution.py:76
Sparse Core Ops, SparseCore 0:
  69.2 113.1 all-reduce.2
  187.8 243.3 all-reduce.4
where the time goes:
time: 465 us
  waiting for transfers between devices  366 us (79%)
  other arithmetic  38.4 us (8%)
  matrix products  28.8 us (6%)
  between operations  14.3 us (3%)
  local copies, waits for them, and re-layouts  14 us (3%)
    psum x1, waiting for transfers between devices, per_device(): gram_matrix = lax.psum(local_gram, ('pole', 'sub'))  247 us
    psum x1, waiting for transfers between devices, per_device(): summed_poles = lax.psum(pole_term, 'pole')  113 us
    dot_general x2, matrix products, apply_blocks(): jnp.einsum('sij,sjv->siv', blocks, fields, precision=precise, preferred_e...  23.2 us
    unnamed x5, other arithmetic  13.9 us
    another operation x3, other arithmetic, per_device(): lower_factor = jnp.linalg.cholesky(gram_matrix)  12.4 us
    another operation x2, other arithmetic, per_device(): lax.linalg.triangular_solve(lower_factor, filtered, left_side=False, lowe...  10.5 us
  transfers between devices with their start and end apart: 4, of which 4 were waited for; matrix products, arithmetic and copies ran while one was open for 0% of the time, Pallas kernels for 0%

commit v1 on v0

--- a/solution.py
+++ b/solution.py
@@ -73,7 +73,7 @@
     local_gram = jnp.dot(
         filtered.T, filtered, precision=precise, preferred_element_type=jnp.float32
     )
-    gram_matrix = lax.psum(local_gram, ("pole", "sub"))
+    gram_matrix = lax.psum(lax.psum(local_gram, "pole"), "sub")
     lower_factor = jnp.linalg.cholesky(gram_matrix)
     total_rows = sub_count * block_len * lax.axis_size("sub")
     solved = lax.linalg.triangular_solve(

time: 465 us -> 536 us (1.15)
  waiting for transfers between devices: 366 us -> 436 us
    psum x1 -> x2, waiting for transfers between devices: 247 us -> 317 us  [per_device(): gram_matrix = lax.psum(lax.psum(local_gram, 'pole'), 'sub')]
  transfers between devices with their start and end apart: 4 -> 5, of which waited for: 4 -> 5; matrix products, arithmetic and copies ran while one was open for 0% -> 0% of each run, Pallas kernels for 0% -> 0%
where the time goes in v1:
time: 536 us; the launch traced here: 535 us
  waiting for transfers between devices  436 us (81%)
  other arithmetic  38.4 us (7%)
  matrix products  28.8 us (5%)
  local copies, waits for them, and re-layouts  14 us (3%)
  between operations  14 us (3%)
    psum x2, waiting for transfers between devices, per_device(): gram_matrix = lax.psum(lax.psum(local_gram, 'pole'), 'sub')  317 us
    psum x1, waiting for transfers between devices, per_device(): summed_poles = lax.psum(pole_term, 'pole')  113 us
    dot_general x2, matrix products, apply_blocks(): jnp.einsum('sij,sjv->siv', blocks, fields, precision=precise, preferred_e...  23.2 us
    unnamed x5, other arithmetic  13.9 us
    another operation x3, other arithmetic, per_device(): lower_factor = jnp.linalg.cholesky(gram_matrix)  12.4 us
  transfers between devices with their start and end apart: 5, of which 5 were waited for; matrix products, arithmetic and copies ran while one was open for 0% of the time, Pallas kernels for 0%

profile of v1, /device:TPU:1, one launch (start us, length us, event | category | flops | bytes accessed | tf_op | source)
XLA Modules:
  0.0 534.8 jit_solution(12055273918858425361)
XLA Ops:
  6.5 0.0 all-reduce.4.cloned.1.call-start
  6.5 1.6 copy.38
  8.1 0.0 copy-done
  8.1 0.1 compare_and_fusion
  8.3 10.6 %fusion.2 = f32[8,512,128]{2,1,0:T(8,128)} fusion(f32[8,512,128]{2,1,0:T(8,128)S(1)} %bitcast.62, f32[1,8,512,512]{3,2,1,0:T(8,128)} %param.7), kind=kOutput, calls=%fused_computation.5 | convolution fusion | flops 3221225472 | bytes 12582912 | tf_op jit(solution)/shard_map/sij,sjv->siv/dot_general | solution.py:27
  18.8 7.0 %gather_fusion = f32[2048,128]{1,0:T(8,128)S(1)} fusion(f32[4096,128]{1,0:T(8,128)} %bitcast.64, s32[2048]{0:T(1024)S(1)} %broadcast_clamp_fusion), kind=kCustom, calls=%fused_computation | custom fusion | bytes 2105344 | tf_op jit(solution)/shard_map/jit(_take)/gather | solution.py:51
  25.9 0.0 slice-start
  25.9 0.0 copy-start.2
  25.9 0.0 copy-start.3
  25.9 0.0 copy-start.1
  25.9 0.0 copy-start.4
  25.9 0.3 broadcast_select_fusion
  26.3 1.1 fusion.27
  27.3 3.2 collective-permute-start.1
  30.5 0.0 collective-permute-start
  30.6 0.0 copy-done.3
  30.6 0.1 multiply_reduce_fusion
  30.7 0.0 copy-done.1
  30.7 0.1 copy.12
  31.5 0.1 and_reduce_fusion
  31.6 5.8 %collective-permute-done.1 = f32[1024,128]{1,0:T(8,128)S(1)} collective-permute-done((f32[1024,128]{1,0:T(8,128)}, f32[1024,128]{1,0:T(8,128)S(1)}, u32[]{:S(2)}, u32[]{:S(2)}) %collective-permute-start.1) | collective-permute-done | bytes 524320 | tf_op jit(solution)/shard_map/ppermute | solution.py:19
  37.4 0.7 convolution_bitcast_fusion
  38.1 0.3 collective-permute-done
  38.4 0.7 convolution_bitcast_fusion.1
  39.0 0.3 maximum_multiply_fusion
  39.4 0.1 fusion.26
  39.5 0.1 copy.16
  39.6 0.1 copy.18
  39.7 6.8 %scatter_fusion = f32[4096,128]{1,0:T(8,128)S(1)} fusion(f32[4096,128]{1,0:T(8,128)S(1)} %copy.38, s32[1024]{0:T(1024)S(1)} %get-tuple-element.18, f32[1024,128]{1,0:T(8,128)S(1)} %bitcast.67), kind=kCustom, calls=%fused_computation.1 | custom fusion | flops 131072 | bytes 1576960
  46.5 7.0 %scatter_fusion.1 = f32[4096,128]{1,0:T(8,128)S(1)} fusion(f32[4096,128]{1,0:T(8,128)S(1)} %scatter_fusion, s32[1024]{0:T(1024)S(1)} %get-tuple-element.17, f32[1024,128]{1,0:T(8,128)S(1)} %bitcast.66), kind=kCustom, calls=%fused_computation.2 | custom fusion | flops 131072 | bytes 1576960
  53.5 12.6 %multiply_bitcast_fusion = f32[8,512,128]{1,2,0:T(8,128)} fusion(f32[8,512,128]{2,1,0:T(8,128)S(1)} %bitcast.63, f32[1,8,512,512]{3,2,1,0:T(8,128)} %param.7, f32[]{:T(128)} %bitcast.61), kind=kOutput, calls=%fused_computation.7 | convolution fusion | flops 3221749760 | bytes 12582916 | tf_op jit(solution)/shard_map/sij,sjv->siv/dot_general | solution.py:27
  66.1 2.9 copy.20
  69.0 0.0 all-reduce.4.cloned.1.call-update
  69.0 0.0 all-reduce.6.cloned.1.call-start
  69.1 113.2 %all-reduce.4.cloned.1.call-done = f32[4096,128]{1,0:T(8,128)} async-done(((f32[4096,128]{1,0:T(8,128)}), f32[4096,128]{1,0:T(8,128)}) %all-reduce.4.cloned.1.call-update) | async-done | bytes 2097168 | tf_op jit(solution)/shard_map/psum | solution.py:69
  182.3 2.2 fusion.9
  184.6 0.0 all-reduce.6.cloned.1.call-update
  184.6 0.0 all-reduce.8.cloned.1.call-start
  184.6 75.5 %all-reduce.6.cloned.1.call-done = f32[128,128]{0,1:T(8,128)} async-done(((f32[128,128]{0,1:T(8,128)}), f32[128,128]{0,1:T(8,128)}) %all-reduce.6.cloned.1.call-update) | async-done | bytes 65552 | tf_op jit(solution)/shard_map/psum | solution.py:76
  260.2 0.0 all-reduce.8.cloned.1.call-update
  260.2 241.4 %all-reduce.8.cloned.1.call-done = f32[128,128]{0,1:T(8,128)} async-done(((f32[128,128]{0,1:T(8,128)}), f32[128,128]{0,1:T(8,128)}) %all-reduce.8.cloned.1.call-update) | async-done | bytes 65552 | tf_op jit(solution)/shard_map/psum | solution.py:76
  501.6 0.9 copy.22
  502.5 0.9 fusion.13
  503.4 11.7 %cholesky.16 = f32[128,128]{1,0:T(8,128)S(1)} custom-call(f32[128,128]{1,0:T(8,128)S(1)} %fusion.13), custom_call_target="Cholesky" | custom-call | tf_op jit(solution)/shard_map/jit(cholesky)/cholesky | solution.py:77
  515.1 0.6 compare_reduce_fusion
  515.8 0.7 fusion.11
  516.4 9.8 %custom-call.6 = f32[1,128,128]{1,2,0:T(8,128)S(1)} custom-call(f32[1,128,128]{2,1,0:T(8,128)S(1)} %fusion.11), custom_call_target="InvertDiagBlocksLowerTriangular" | custom-call | tf_op jit(solution)/shard_map/triangular_solve | solution.py:79
  526.3 2.0 convolution_multiply_fusion
  (14 shorter events, 0.1 us)
Async XLA Ops:
  6.5 1.6 copy-start
  6.5 175.8 %all-reduce.4.cloned.1.call-start = ((), (), s32[]{:S(2)}) async-start(), calls=%async_computation | async-start | bytes 4194304 | tf_op jit(solution)/shard_map/psum | solution.py:69
  25.9 4.7 slice-start
  25.9 4.7 copy-start.2
  25.9 4.7 copy-start.3
  25.9 4.8 copy-start.1
  25.9 5.6 %copy-start.4 = (s32[2]{0:T(128)S(1)}, s32[2]{0:T(128)}, u32[]{:S(2)}) copy-start(s32[2]{0:T(128)} %constant.98) | copy-start | bytes 28
  27.3 10.1 %collective-permute-start.1 = (f32[1024,128]{1,0:T(8,128)}, f32[1024,128]{1,0:T(8,128)S(1)}, u32[]{:S(2)}, u32[]{:S(2)}) collective-permute-start(f32[1024,128]{1,0:T(8,128)} %get-tuple-element.14), channel_id=1, source_target_pairs={{1,0},{2,1},{3,2},{4,3},{5,4},{6,5},{7,6},{8,7},{9,8},{10,9},{11,1... | collective-permute-start | bytes 1572872 | tf_op jit(solution)/shard_map/ppermute | solution.py:19
  30.5 7.8 %collective-permute-start = (f32[1024,128]{1,0:T(8,128)}, f32[1024,128]{1,0:T(8,128)S(1)}, u32[]{:S(2)}, u32[]{:S(2)}) collective-permute-start(f32[1024,128]{1,0:T(8,128)} %get-tuple-element.13), channel_id=1, source_target_pairs={{0,1},{1,2},{2,3},{3,4},{4,5},{5,6},{6,7},{7,8},{8,9},{9,10},{10,1... | collective-permute-start | bytes 1572872 | tf_op jit(solution)/shard_map/ppermute | solution.py:17
  69.0 191.1 %all-reduce.6.cloned.1.call-start = ((), (), s32[]{:S(2)}) async-start(), calls=%async_computation.1 | async-start | bytes 131072 | tf_op jit(solution)/shard_map/psum | solution.py:76
  184.6 317.0 %all-reduce.8.cloned.1.call-start = ((), (), s32[]{:S(2)}) async-start(), calls=%async_computation.2 | async-start | bytes 131072 | tf_op jit(solution)/shard_map/psum | solution.py:76
Sparse Core Ops, SparseCore 0:
  69.2 113.1 all-reduce.3
  184.9 75.2 all-reduce.5
  262.8 238.7 all-reduce.7
